TPU v7x, 32 devices: a whole 2x2x4 slice. The times are simulated.
32 devices in a mesh: cond: 4 (over y, x), slab: 8 (over z, core).
Axes of the slice: x: 2, y: 2, z: 4, core: 2. Of those that a mesh axis runs over, the one named last changes fastest.
Arguments:
- mask_pixels: int32 [2048, 2048], P('slab'), may hold values 0 or 1
- target_bits: int32 [2048, 2048], P('slab'), may hold values 0 or 1
- perturb: float32 [2048, 2048], P('slab'), may hold values from -1.5 to 1.5
- diffusivity: float32 [2048, 2048], P('slab'), may hold values from 0.03 to 0.24
- kernels: float32 [4, 8, 2, 128, 128], P('cond'), may hold values from -6 to 6
- cond_ids: int32 [4], P('cond'), may hold values from 0 to 15
- dose_table: float32 [16], replicated, may hold values from 0.7 to 1.3
Outputs:
- mask_grad: float32 [2048, 2048], P('slab')
All inputs are finite; a program needn't handle non-finite values. No bound on the sum of `mask_pixels` or of `target_bits` on one device may be relied on, other than what follows from the above.
Results may differ from a plain program's by a relative error of at most 0.0003.
Values sent between devices are 32-bit elements; how exact they have to be, the bound alone decides.
A program may use at most 192 MiB of HBM per device.

v0:
```python
import functools
import math

import jax
import jax.numpy as jnp
import numpy as np
from jax import lax
from jax.experimental import pallas as pl
from jax.experimental.pallas import tpu as pltpu
from jax.sharding import PartitionSpec as P

STEPS = 4
HALO = 2 * STEPS

steepness = 4.0
threshold = 1.0
theta_scale = 2.5

f32 = jnp.float32
bf16 = jnp.bfloat16
VMEM = pl.BlockSpec(memory_space=pltpu.VMEM)
SMEM = pl.BlockSpec(memory_space=pltpu.SMEM)
NN = (((1,), (0,)), ((), ()))
NT = (((1,), (1,)), ((), ()))
TN = (((0,), (0,)), ((), ()))


def split_np(table):
    high = table.astype(bf16)
    low = (table - high.astype(np.float64)).astype(bf16)
    return jnp.asarray(high), jnp.asarray(low)


def coarse_tables(band):
    points = 2 * band
    turns = np.arange(points)[:, None] * (np.arange(band)[None, :] - band // 2) % points
    angle = turns * (2.0 * math.pi / points)
    cos, sin = np.cos(angle), np.sin(angle)
    return np.concatenate(
        [np.concatenate([cos, -sin], 1), np.concatenate([sin, cos], 1)], 0
    )


def interpolation_table(length, band):
    points = 2 * band
    fine = np.arange(-HALO, length + HALO)
    scale = length // points
    offset = (fine[:, None] - scale * np.arange(points)[None, :]) % length
    freq = np.arange(1, band)
    profile = 1.0 + 2.0 * np.cos(
        (np.arange(length)[:, None] * freq[None, :] % length) * (2.0 * math.pi / length)
    ).sum(1)
    return profile[offset] / points


def angle_parts(length, band, inner):
    freq = np.arange(band) - band // 2
    fine = (np.arange(inner)[:, None] * freq % length) * (2.0 * math.pi / length)
    jump = (np.arange(length // inner)[:, None] * inner * freq % length) * (
        2.0 * math.pi / length
    )
    small = np.stack([np.cos(fine), np.sin(fine)]).astype(np.float32)
    large = np.stack([np.cos(jump), np.sin(jump)]).astype(np.float32)
    return jnp.asarray(small), jnp.asarray(large)


def halves(value):
    high = value.astype(bf16)
    return high, (value - high.astype(f32)).astype(bf16)


def dot3(left, right, dims=NN):
    go = lambda a, b: lax.dot_general(a, b, dims, preferred_element_type=f32)
    return go(left[0], right[0]) + (go(left[0], right[1]) + go(left[1], right[0]))


def project_kernel(mask, perturb, small, large, trans, tab_h, tab_l, band_out, acc):
    rows, length = mask.shape
    band = small.shape[2]
    inner = small.shape[1]
    cos_b, sin_b = small[0], small[1]

    @pl.loop(0, length // inner)
    def _(step):
        cos_a = large[0, pl.ds(step, 1), :]
        sin_a = large[1, pl.ds(step, 1), :]
        at = pl.ds(pl.multiple_of(step * inner, inner), inner)
        for part, value in (
            (0, cos_a * cos_b - sin_a * sin_b),
            (1, -(sin_a * cos_b + cos_a * sin_b)),
        ):
            high, low = halves(value)
            tab_h[at, part * band : (part + 1) * band] = high
            tab_l[at, part * band : (part + 1) * band] = low

    acc[...] = jnp.zeros_like(acc)
    wide = 256

    @pl.loop(0, length // wide)
    def _(step):
        at = pl.ds(pl.multiple_of(step * wide, wide), wide)
        theta = theta_scale * (2.0 * mask[:, at].astype(f32) - 1.0) + perturb[:, at]
        value = jnp.tanh(0.5 * theta)
        trans[:, at] = value
        acc[...] += dot3(halves(value), (tab_h[at, :], tab_l[at, :]))

    mine = pl.ds(pl.multiple_of(lax.axis_index("slab") * rows, rows), rows)
    mixed = dot3((tab_h[mine, :], tab_l[mine, :]), halves(acc[...] / length), TN)
    band_out[0:band, :] = mixed[0:band, 0:band] - mixed[band:, band:]
    band_out[band:, :] = mixed[0:band, band:] + mixed[band:, 0:band]


def bake_sweep(field, vert, horiz, row_mask):
    total, length = field.shape
    chunks = total // 8

    def body(index, carry):
        at = pl.ds(pl.multiple_of(index * 8, 8), 8)
        after = pl.ds(pl.multiple_of(jnp.minimum(index + 1, chunks - 1) * 8, 8), 8)
        here = field[at, :]
        there = field[after, :]
        last = row_mask == 7
        below = jnp.where(last, pltpu.roll(there, 7, 0), pltpu.roll(here, 7, 0))
        flow = vert[at, :] * (below - here)
        rolled = pltpu.roll(flow, 1, 0)
        above = jnp.where(row_mask == 0, carry, rolled)
        side = horiz[at, :] * (pltpu.roll(here, length - 1, 1) - here)
        field[at, :] = here + (flow - above) + (side - pltpu.roll(side, 1, 1))
        return rolled

    lax.fori_loop(0, chunks, body, jnp.zeros((8, length), f32))


def image_kernel(
    band_in, kern, dose, diff, target, lh, ll, th, tl, wh, wl, out,
    ah, al, mid, fields, coarse, field, vert, horiz, zh, zl, grad, qh, ql,
):
    count, _, band, _ = kern.shape
    total, length = diff.shape
    rows = total - 2 * HALO
    points = 2 * band
    level = dose[0, 0]
    first = pl.multiple_of(lax.axis_index("slab") * rows, rows)
    row_mask = lax.broadcasted_iota(jnp.int32, (8, length), 0)
    chunks = total // 8

    @pl.loop(0, chunks)
    def _(index):
        at = pl.ds(pl.multiple_of(index * 8, 8), 8)
        after = pl.ds(pl.multiple_of(jnp.minimum(index + 1, chunks - 1) * 8, 8), 8)
        here = diff[at, :]
        below = jnp.where(
            row_mask == 7, pltpu.roll(diff[after, :], 7, 0), pltpu.roll(here, 7, 0)
        )
        vert[at, :] = 0.5 * (here + below)
        horiz[at, :] = 0.5 * (here + pltpu.roll(here, length - 1, 1))

    real, imag = band_in[0:band, :], band_in[band:, :]
    for k in range(count):
        cols = slice(k * band, (k + 1) * band)
        kr, ki = kern[k, 0], kern[k, 1]
        ah[0:band, cols], al[0:band, cols] = halves(kr * real - ki * imag)
        ah[band:, cols], al[band:, cols] = halves(kr * imag + ki * real)

    @pl.loop(0, count // 2)
    def _(pair):
        at = pl.ds(pl.multiple_of(pair * points, points), points)
        mid[:, at] = dot3((lh[...], ll[...]), (ah[:, at], al[:, at]))

    coarse[...] = jnp.zeros_like(coarse)

    @pl.loop(0, count)
    def _(k):
        at = pl.ds(pl.multiple_of(k * band, band), band)
        block = jnp.concatenate([mid[0:points, at], mid[points:, at]], axis=1)
        value = dot3(halves(block), (th[...], tl[...])) * (1.0 / band)
        fields[k] = value
        re, im = value[:, :points], value[:, points:]
        coarse[...] += re * re + im * im

    near = pl.ds(first, total)
    zh[...], zl[...] = halves(
        dot3((wh[near, :], wl[near, :]), halves(coarse[...] * (level / count)))
    )
    wide = 256

    @pl.loop(0, length // wide)
    def _(step):
        at = pl.ds(pl.multiple_of(step * wide, wide), wide)
        src = pl.ds(pl.multiple_of(step * wide + HALO, HALO), wide)
        field[:, at] = dot3((zh[...], zl[...]), (wh[src, :], wl[src, :]), NT)

    @pl.loop(0, STEPS)
    def _(sweep):
        bake_sweep(field, vert, horiz, row_mask)

    @pl.loop(0, chunks)
    def _(index):
        at = pl.ds(pl.multiple_of(index * 8, 8), 8)
        resist = jax.nn.sigmoid(steepness * (field[at, :] - threshold))
        field[at, :] = (
            steepness * (resist - target[at, :].astype(f32)) * resist * (1.0 - resist)
        )

    @pl.loop(0, STEPS)
    def _(sweep):
        bake_sweep(field, vert, horiz, row_mask)

    grad[...] = jnp.zeros_like(grad)

    @pl.loop(0, length // wide)
    def _(step):
        at = pl.ds(pl.multiple_of(step * wide, wide), wide)
        src = pl.ds(pl.multiple_of(step * wide + HALO, HALO), wide)
        grad[...] += dot3(
            halves(field[HALO : HALO + rows, at]), (wh[src, :], wl[src, :])
        )

    inside = pl.ds(pl.multiple_of(first + HALO, HALO), rows)
    spread = dot3((wh[inside, :], wl[inside, :]), halves(grad[...]), TN)
    coarse[...] = spread * (2.0 * level / count / band)

    @pl.loop(0, count)
    def _(k):
        at = pl.ds(pl.multiple_of(k * band, band), band)
        weight = coarse[...]
        block = fields[k] * jnp.concatenate([weight, weight], axis=1)
        back = dot3(halves(block), (lh[...], ll[...]))
        qh[0:points, at], ql[0:points, at] = halves(back[:, :band])
        qh[points:, at], ql[points:, at] = halves(back[:, band:])

    @pl.loop(0, count // 2)
    def _(pair):
        at = pl.ds(pl.multiple_of(pair * points, points), points)
        mid[0:points, at] = dot3((th[...], tl[...]), (qh[:, at], ql[:, at]))

    sum_re = jnp.zeros((band, band), f32)
    sum_im = jnp.zeros((band, band), f32)
    for k in range(count):
        cols = slice(k * band, (k + 1) * band)
        kr, ki = kern[k, 0], kern[k, 1]
        gr, gi = mid[0:band, cols], mid[band:points, cols]
        sum_re += kr * gr + ki * gi
        sum_im += kr * gi - ki * gr
    out[0:band, :] = sum_re
    out[band:, :] = sum_im


def final_kernel(grad, trans, tab_h, tab_l, out, bh, bl):
    rows, length = trans.shape
    band = grad.shape[1]
    top, low = grad[0:band, :], grad[band:, :]
    matrix = jnp.concatenate(
        [jnp.concatenate([top, low], 1), jnp.concatenate([low, -top], 1)], 0
    )
    mine = pl.ds(pl.multiple_of(lax.axis_index("slab") * rows, rows), rows)
    bh[...], bl[...] = halves(
        dot3((tab_h[mine, :], tab_l[mine, :]), halves(matrix)) * (0.5 / length)
    )
    wide = 256

    @pl.loop(0, length // wide)
    def _(step):
        at = pl.ds(pl.multiple_of(step * wide, wide), wide)
        value = dot3((bh[...], bl[...]), (tab_h[at, :], tab_l[at, :]), NT)
        t = trans[:, at]
        out[:, at] = value * (1.0 - t * t)


def with_halo(cells, width):
    count = lax.axis_size("slab")
    head = cells[:width]
    tail = cells[cells.shape[0] - width :]
    return jnp.concatenate(
        [
            lax.ppermute(tail, "slab", [(i, (i + 1) % count) for i in range(count)]),
            cells,
            lax.ppermute(head, "slab", [((i + 1) % count, i) for i in range(count)]),
        ],
        axis=0,
    )


def shape(dims, kind=f32):
    return jax.ShapeDtypeStruct(dims, kind)


def shards(mask_pixels, target_bits, perturb, diffusivity, kernels, cond_ids, dose_table):
    rows, length = mask_pixels.shape
    count, band = kernels.shape[1], kernels.shape[-1]
    points = 2 * band
    total = rows + 2 * HALO
    params = pltpu.CompilerParams(vmem_limit_bytes=60 * 1024 * 1024)
    small, large = angle_parts(length, band, 64)
    left = coarse_tables(band)
    lh, ll = split_np(left)
    th, tl = split_np(np.ascontiguousarray(left.T))
    wh, wl = split_np(interpolation_table(length, band))
    trans, tab_h, tab_l, local = pl.pallas_call(
        project_kernel,
        out_shape=(
            shape((rows, length)),
            shape((length, points), bf16),
            shape((length, points), bf16),
            shape((points, band)),
        ),
        in_specs=[VMEM] * 4,
        out_specs=(VMEM,) * 4,
        scratch_shapes=[pltpu.VMEM((rows, points), f32)],
        compiler_params=params,
        name="project",
    )(mask_pixels, perturb, small, large)
    mask_band = lax.psum(local, "slab")
    levels = jnp.arange(dose_table.shape[0], dtype=jnp.int32)
    dose = jnp.sum(dose_table * (levels == cond_ids[0]).astype(f32)).reshape(1, 1)
    diff = with_halo(diffusivity, HALO)
    target = with_halo(target_bits, HALO)
    part = pl.pallas_call(
        image_kernel,
        out_shape=shape((points, band)),
        in_specs=[VMEM] * 2 + [SMEM] + [VMEM] * 8,
        out_specs=VMEM,
        scratch_shapes=[
            pltpu.VMEM((points, count * band), bf16),
            pltpu.VMEM((points, count * band), bf16),
            pltpu.VMEM((2 * points, count * band), f32),
            pltpu.VMEM((count, points, 2 * points), f32),
            pltpu.VMEM((points, points), f32),
            pltpu.VMEM((total, length), f32),
            pltpu.VMEM((total, length), f32),
            pltpu.VMEM((total, length), f32),
            pltpu.VMEM((total, points), bf16),
            pltpu.VMEM((total, points), bf16),
            pltpu.VMEM((rows, points), f32),
            pltpu.VMEM((2 * points, count * band), bf16),
            pltpu.VMEM((2 * points, count * band), bf16),
        ],
        compiler_params=params,
        name="image",
    )(mask_band, kernels[0], dose, diff, target, lh, ll, th, tl, wh, wl)
    grad = lax.psum(part, ("cond", "slab"))
    return pl.pallas_call(
        final_kernel,
        out_shape=shape((rows, length)),
        in_specs=[VMEM] * 4,
        out_specs=VMEM,
        scratch_shapes=[
            pltpu.VMEM((rows, points), bf16),
            pltpu.VMEM((rows, points), bf16),
        ],
        compiler_params=params,
        name="final",
    )(grad, trans, tab_h, tab_l)


def solution(mesh):
    placed = (
        P("slab", None),
        P("slab", None),
        P("slab", None),
        P("slab", None),
        P("cond", None, None, None, None),
        P("cond"),
        P(),
    )
    return jax.shard_map(
        shards, mesh=mesh, in_specs=placed, out_specs=P("slab", None), check_vma=False
    )
```

profile of v0, /device:TPU:0, one launch (start us, length us, event | category | flops | bytes accessed | tf_op | source)
XLA Modules:
  0.0 275.8 jit_solution(11749042894639773005)
XLA Ops:
  6.5 0.0 copy-start
  6.5 0.0 copy-start.2
  6.5 0.0 all-reduce.3.cloned.1.call-start
  6.5 7.2 %project.1 = (f32[256,2048]{1,0:T(8,128)}, bf16[2048,256]{1,0:T(8,128)(2,1)}, bf16[2048,256]{1,0:T(8,128)(2,1)}, f32[256,128]{1,0:T(8,128)}) custom-call(s32[256,2048]{1,0:T(8,128)} %mask.1, f32[256,2048]{1,0:T(8,128)} %perturb.1, f32[2,64,128]{2,1,0:T(8,128)} %constant.19.clone.small, f32[2,32,128]{2,1,0:T(8,128)} %constant.20.clone.large), custom_call_target="tpu_custom_call" | custom-call | tf_op jit(solution)/shard_map/project/pallas_call | solution.py:299
  13.7 0.0 all-reduce.3.cloned.1.call-update
  13.7 0.0 all-reduce.5.cloned.1.call-start
  13.8 0.0 copy-done
  13.8 0.5 collective-permute-start.2
  14.4 4.1 %collective-permute-start.3 = (s32[8,2048]{1,0:T(8,128)S(1)}, s32[8,2048]{1,0:T(8,128)S(1)}, u32[]{:S(2)}, u32[]{:S(2)}) collective-permute-start(s32[8,2048]{1,0:T(8,128)S(1)} %get-tuple-element.14), channel_id=1, source_target_pairs={{1,0},{2,1},{3,2},{4,3},{5,4},{6,5},{7,6},{0,7},{9,8},{10,9},{11,1... | collective-permute-start | bytes 196616 | tf_op jit(solution)/shard_map/ppermute | solution.py:278
  18.5 0.9 fusion.2
  19.3 0.1 collective-permute-start
  19.4 3.5 %collective-permute-start.1 = (f32[8,2048]{1,0:T(8,128)S(1)}, f32[8,2048]{1,0:T(8,128)S(1)}, u32[]{:S(2)}, u32[]{:S(2)}) collective-permute-start(f32[8,2048]{1,0:T(8,128)S(1)} %get-tuple-element.16), channel_id=1, source_target_pairs={{1,0},{2,1},{3,2},{4,3},{5,4},{6,5},{7,6},{0,7},{9,8},{10,9},{11,1... | collective-permute-start | bytes 196616 | tf_op jit(solution)/shard_map/ppermute | solution.py:278
  23.6 0.0 copy-done.2
  23.6 0.6 fusion
  24.2 0.0 copy-start.1
  24.2 0.0 collective-permute-done.2
  24.2 0.0 collective-permute-done.3
  24.2 1.5 pad_add_fusion.target
  25.7 0.0 collective-permute-done
  25.7 0.0 collective-permute-done.1
  25.7 0.9 copy-done.1
  26.6 1.5 pad_maximum_fusion.diff
  28.2 43.4 %all-reduce.3.cloned.1.call-done.band_in = f32[256,128]{1,0:T(8,128)} async-done(((f32[256,128]{1,0:T(8,128)}), f32[256,128]{1,0:T(8,128)}) %all-reduce.3.cloned.1.call-update) | async-done | bytes 131088 | tf_op jit(solution)/shard_map/psum | solution.py:313
  71.6 67.3 %image.1 = f32[256,128]{1,0:T(8,128)} custom-call(f32[256,128]{1,0:T(8,128)} %all-reduce.3.cloned.1.call-done.band_in, f32[8,2,128,128]{3,2,1,0:T(8,128)} %bitcast.4, f32[1,1]{1,0:T(1,128)} %bitcast.2.dose, f32[272,2048]{1,0:T(8,128)} %pad_maximum_fusion.diff, s32[272,2048]{1,0:T(8,128)} %pad_add_fusion.target, bf16[512,256]{1,0:T(8,128)(2,1)} %constant.21.clone.lh, ...), custom_call_target="tpu_custom_call" | custom-call | tf_op jit(solution)/shard_map/image/pallas_call | solution.py:318
  139.0 0.0 all-reduce.5.cloned.1.call-update
  139.0 123.7 %all-reduce.5.cloned.1.call-done.grad = f32[256,128]{1,0:T(8,128)} async-done(((f32[256,128]{1,0:T(8,128)}), f32[256,128]{1,0:T(8,128)}) %all-reduce.5.cloned.1.call-update) | async-done | bytes 131088 | tf_op jit(solution)/shard_map/psum | solution.py:341
  262.7 6.2 %final.1 = f32[256,2048]{1,0:T(8,128)} custom-call(f32[256,128]{1,0:T(8,128)} %all-reduce.5.cloned.1.call-done.grad, f32[256,2048]{1,0:T(8,128)} %get-tuple-element.10.trans, bf16[2048,256]{1,0:T(8,128)(2,1)} %get-tuple-element.11.tab_h, bf16[2048,256]{1,0:T(8,128)(2,1)} %get-tuple-element.12.tab_l), custom_call_target="tpu_custom_call" | custom-call | tf_op jit(solution)/shard_map/final/pallas_call | solution.py:342
  (1 shorter events, 0.0 us)
Async XLA Ops:
  6.5 7.3 %copy-start = (s32[256,2048]{1,0:T(8,128)S(1)}, s32[256,2048]{1,0:T(8,128)}, u32[]{:S(2)}) copy-start(s32[256,2048]{1,0:T(8,128)} %param.16) | copy-start | bytes 6291460
  6.5 17.1 %copy-start.2 = (f32[16]{0:T(128)S(1)}, f32[16]{0:T(128)}, u32[]{:S(2)}) copy-start(f32[16]{0:T(128)} %param.21) | copy-start | bytes 196
  6.5 65.1 %all-reduce.3.cloned.1.call-start = ((), (), s32[]{:S(2)}) async-start(), calls=%async_computation | async-start | bytes 262144 | tf_op jit(solution)/shard_map/psum | solution.py:313
  13.7 249.0 %all-reduce.5.cloned.1.call-start = ((), (), s32[]{:S(2)}) async-start(), calls=%async_computation.1 | async-start | bytes 262144 | tf_op jit(solution)/shard_map/psum | solution.py:341
  13.8 10.4 %collective-permute-start.2 = (s32[8,2048]{1,0:T(8,128)S(1)}, s32[8,2048]{1,0:T(8,128)S(1)}, u32[]{:S(2)}, u32[]{:S(2)}) collective-permute-start(s32[8,2048]{1,0:T(8,128)S(1)} %get-tuple-element.13), channel_id=1, source_target_pairs={{0,1},{1,2},{2,3},{3,4},{4,5},{5,6},{6,7},{7,0},{8,9},{9,10},{10,1... | collective-permute-start | bytes 196616 | tf_op jit(solution)/shard_map/ppermute | solution.py:276
  14.4 9.9 %collective-permute-start.3 = (s32[8,2048]{1,0:T(8,128)S(1)}, s32[8,2048]{1,0:T(8,128)S(1)}, u32[]{:S(2)}, u32[]{:S(2)}) collective-permute-start(s32[8,2048]{1,0:T(8,128)S(1)} %get-tuple-element.14), channel_id=1, source_target_pairs={{1,0},{2,1},{3,2},{4,3},{5,4},{6,5},{7,6},{0,7},{9,8},{10,9},{11,1... | collective-permute-start | bytes 196616 | tf_op jit(solution)/shard_map/ppermute | solution.py:278
  19.3 6.4 %collective-permute-start = (f32[8,2048]{1,0:T(8,128)S(1)}, f32[8,2048]{1,0:T(8,128)S(1)}, u32[]{:S(2)}, u32[]{:S(2)}) collective-permute-start(f32[8,2048]{1,0:T(8,128)S(1)} %get-tuple-element.15), channel_id=1, source_target_pairs={{0,1},{1,2},{2,3},{3,4},{4,5},{5,6},{6,7},{7,0},{8,9},{9,10},{10,1... | collective-permute-start | bytes 196616 | tf_op jit(solution)/shard_map/ppermute | solution.py:276
  19.4 6.3 %collective-permute-start.1 = (f32[8,2048]{1,0:T(8,128)S(1)}, f32[8,2048]{1,0:T(8,128)S(1)}, u32[]{:S(2)}, u32[]{:S(2)}) collective-permute-start(f32[8,2048]{1,0:T(8,128)S(1)} %get-tuple-element.16), channel_id=1, source_target_pairs={{1,0},{2,1},{3,2},{4,3},{5,4},{6,5},{7,6},{0,7},{9,8},{10,9},{11,1... | collective-permute-start | bytes 196616 | tf_op jit(solution)/shard_map/ppermute | solution.py:278
  24.2 2.4 copy-start.1
Sparse Core Ops, SparseCore 0:
  13.9 57.6 all-reduce.2
  139.1 123.5 all-reduce.4
where the time goes:
time: 276 us
  waiting for transfers between devices  167 us (61%)
  Pallas kernels  80.8 us (29%)
  between operations  14.1 us (5%)
  starting transfers between devices  8.27 us (3%)
  other arithmetic  3.64 us (1%)
    psum x1, waiting for transfers between devices, shards(): grad = lax.psum(part, ('cond', 'slab'))  124 us
    pallas_call x1, Pallas kernels, shards(): pl.pallas_call(image_kernel, out_shape=shape((points, band)), in_specs=[V...  67.3 us
    psum x1, waiting for transfers between devices, shards(): mask_band = lax.psum(local, 'slab')  43.4 us
    ppermute x2, starting transfers between devices, with_halo(): lax.ppermute(head, 'slab', [((i + 1) % count, i) for i in range(count)])  7.62 us
    pallas_call x1, Pallas kernels, shards(): pl.pallas_call(project_kernel, out_shape=(shape((rows, length)), shape((l...  7.18 us
    pallas_call x1, Pallas kernels, shards(): pl.pallas_call(final_kernel, out_shape=shape((rows, length)), in_specs=[V...  6.23 us
  transfers between devices with their start and end apart: 6, of which 2 were waited for; matrix products, arithmetic and copies ran while one was open for 2% of the time, Pallas kernels for 0%

commit v1 on v0

--- a/solution.py
+++ b/solution.py
@@ -19,6 +19,8 @@
 f32 = jnp.float32
 bf16 = jnp.bfloat16
 VMEM = pl.BlockSpec(memory_space=pltpu.VMEM)
+ANY = pl.BlockSpec(memory_space=pl.ANY)
+MESH = pl.DeviceIdType.MESH
 SMEM = pl.BlockSpec(memory_space=pltpu.SMEM)
 NN = (((1,), (0,)), ((), ()))
 NT = (((1,), (1,)), ((), ()))
@@ -110,50 +112,63 @@
     band_out[band:, :] = mixed[0:band, band:] + mixed[band:, 0:band]
 
 
-def bake_sweep(field, vert, horiz, row_mask):
-    total, length = field.shape
+def bake_sweep(source, dest, coeffs, row_mask):
+    east, west, north, south, middle = coeffs
+    total, length = middle.shape
     chunks = total // 8
-
-    def body(index, carry):
-        at = pl.ds(pl.multiple_of(index * 8, 8), 8)
-        after = pl.ds(pl.multiple_of(jnp.minimum(index + 1, chunks - 1) * 8, 8), 8)
-        here = field[at, :]
-        there = field[after, :]
-        last = row_mask == 7
-        below = jnp.where(last, pltpu.roll(there, 7, 0), pltpu.roll(here, 7, 0))
-        flow = vert[at, :] * (below - here)
-        rolled = pltpu.roll(flow, 1, 0)
-        above = jnp.where(row_mask == 0, carry, rolled)
-        side = horiz[at, :] * (pltpu.roll(here, length - 1, 1) - here)
-        field[at, :] = here + (flow - above) + (side - pltpu.roll(side, 1, 1))
-        return rolled
-
-    lax.fori_loop(0, chunks, body, jnp.zeros((8, length), f32))
+    unroll = max(d for d in range(1, 18) if chunks % d == 0)
+
+    @pl.loop(0, chunks // unroll)
+    def _(block):
+        for inner in range(unroll):
+            index = block * unroll + inner
+            at = pl.ds(pl.multiple_of(index * 8, 8), 8)
+            put = pl.ds(pl.multiple_of(index * 8 + 8, 8), 8)
+            after = pl.ds(pl.multiple_of(index * 8 + 16, 8), 8)
+            here = source[put, :]
+            above = jnp.where(row_mask == 0, pltpu.roll(source[at, :], 1, 0), pltpu.roll(here, 1, 0))
+            below = jnp.where(row_mask == 7, pltpu.roll(source[after, :], 7, 0), pltpu.roll(here, 7, 0))
+            dest[put, :] = (
+                middle[at, :] * here
+                + (north[at, :] * above + south[at, :] * below)
+                + (
+                    east[at, :] * pltpu.roll(here, length - 1, 1)
+                    + west[at, :] * pltpu.roll(here, 1, 1)
+                )
+            )
 
 
 def image_kernel(
-    band_in, kern, dose, diff, target, lh, ll, th, tl, wh, wl, out,
-    ah, al, mid, fields, coarse, field, vert, horiz, zh, zl, grad, qh, ql,
+    band_in, kern, ids, table, diff, target, diff_halo, target_halo, lh, ll, wh, wl, out,
+    ah, al, mid, fields, coarse, field, other, east, west, north, south, middle,
+    zh, zl, grad, qh, ql, th, tl, cells, goal, sems,
 ):
     count, _, band, _ = kern.shape
-    total, length = diff.shape
-    rows = total - 2 * HALO
+    rows, length = diff.shape
+    total = rows + 2 * HALO
     points = 2 * band
-    level = dose[0, 0]
+    level = table[ids[0]]
     first = pl.multiple_of(lax.axis_index("slab") * rows, rows)
     row_mask = lax.broadcasted_iota(jnp.int32, (8, length), 0)
     chunks = total // 8
-
-    @pl.loop(0, chunks)
-    def _(index):
-        at = pl.ds(pl.multiple_of(index * 8, 8), 8)
-        after = pl.ds(pl.multiple_of(jnp.minimum(index + 1, chunks - 1) * 8, 8), 8)
-        here = diff[at, :]
-        below = jnp.where(
-            row_mask == 7, pltpu.roll(diff[after, :], 7, 0), pltpu.roll(here, 7, 0)
-        )
-        vert[at, :] = 0.5 * (here + below)
-        horiz[at, :] = 0.5 * (here + pltpu.roll(here, length - 1, 1))
+    coeffs = (east, west, north, south, middle)
+
+    loads = [
+        pltpu.make_async_copy(diff, cells.at[pl.ds(8 + HALO, rows)], sems.at[0]),
+        pltpu.make_async_copy(diff_halo.at[0], cells.at[pl.ds(8, HALO)], sems.at[1]),
+        pltpu.make_async_copy(diff_halo.at[1], cells.at[pl.ds(8 + HALO + rows, HALO)], sems.at[2]),
+        pltpu.make_async_copy(target, goal.at[pl.ds(HALO, rows)], sems.at[3]),
+        pltpu.make_async_copy(target_halo.at[0], goal.at[pl.ds(0, HALO)], sems.at[4]),
+        pltpu.make_async_copy(target_halo.at[1], goal.at[pl.ds(HALO + rows, HALO)], sems.at[5]),
+    ]
+    for load in loads:
+        load.start()
+    blank = jnp.zeros((8, length), f32)
+    for ref in (cells, field, other):
+        ref[0:8, :] = blank
+        ref[total + 8 : total + 16, :] = blank
+    th[...] = lh[...].astype(f32).T.astype(bf16)
+    tl[...] = ll[...].astype(f32).T.astype(bf16)
 
     real, imag = band_in[0:band, :], band_in[band:, :]
     for k in range(count):
@@ -188,23 +203,46 @@
     def _(step):
         at = pl.ds(pl.multiple_of(step * wide, wide), wide)
         src = pl.ds(pl.multiple_of(step * wide + HALO, HALO), wide)
-        field[:, at] = dot3((zh[...], zl[...]), (wh[src, :], wl[src, :]), NT)
-
-    @pl.loop(0, STEPS)
-    def _(sweep):
-        bake_sweep(field, vert, horiz, row_mask)
+        field[8 : 8 + total, at] = dot3((zh[...], zl[...]), (wh[src, :], wl[src, :]), NT)
+
+    for load in loads:
+        load.wait()
 
     @pl.loop(0, chunks)
     def _(index):
         at = pl.ds(pl.multiple_of(index * 8, 8), 8)
-        resist = jax.nn.sigmoid(steepness * (field[at, :] - threshold))
-        field[at, :] = (
-            steepness * (resist - target[at, :].astype(f32)) * resist * (1.0 - resist)
-        )
-
-    @pl.loop(0, STEPS)
-    def _(sweep):
-        bake_sweep(field, vert, horiz, row_mask)
+        put = pl.ds(pl.multiple_of(index * 8 + 8, 8), 8)
+        after = pl.ds(pl.multiple_of(index * 8 + 16, 8), 8)
+        here = cells[put, :]
+        above = jnp.where(row_mask == 0, pltpu.roll(cells[at, :], 1, 0), pltpu.roll(here, 1, 0))
+        below = jnp.where(row_mask == 7, pltpu.roll(cells[after, :], 7, 0), pltpu.roll(here, 7, 0))
+        c_e = 0.5 * (here + pltpu.roll(here, length - 1, 1))
+        c_w = 0.5 * (here + pltpu.roll(here, 1, 1))
+        c_n = 0.5 * (here + above)
+        c_s = 0.5 * (here + below)
+        east[at, :] = c_e
+        west[at, :] = c_w
+        north[at, :] = c_n
+        south[at, :] = c_s
+        middle[at, :] = 1.0 - ((c_e + c_w) + (c_n + c_s))
+
+    @pl.loop(0, 2)
+    def _(bake):
+        @pl.loop(0, STEPS // 2)
+        def _(pair):
+            bake_sweep(field, other, coeffs, row_mask)
+            bake_sweep(other, field, coeffs, row_mask)
+
+        @pl.when(bake == 0)
+        def _():
+            @pl.loop(0, chunks)
+            def _(index):
+                at = pl.ds(pl.multiple_of(index * 8, 8), 8)
+                put = pl.ds(pl.multiple_of(index * 8 + 8, 8), 8)
+                resist = jax.nn.sigmoid(steepness * (field[put, :] - threshold))
+                field[put, :] = (
+                    steepness * (resist - goal[at, :].astype(f32)) * resist * (1.0 - resist)
+                )
 
     grad[...] = jnp.zeros_like(grad)
 
@@ -213,7 +251,7 @@
         at = pl.ds(pl.multiple_of(step * wide, wide), wide)
         src = pl.ds(pl.multiple_of(step * wide + HALO, HALO), wide)
         grad[...] += dot3(
-            halves(field[HALO : HALO + rows, at]), (wh[src, :], wl[src, :])
+            halves(field[8 + HALO : 8 + HALO + rows, at]), (wh[src, :], wl[src, :])
         )
 
     inside = pl.ds(pl.multiple_of(first + HALO, HALO), rows)
@@ -267,18 +305,142 @@
         out[:, at] = value * (1.0 - t * t)
 
 
-def with_halo(cells, width):
+def sum_kernel(axes, with_edges, *refs):
+    if with_edges:
+        part, diff, target, out, diff_halo, target_halo = refs[:6]
+        refs = refs[6:]
+        edge_send, edge_recv = refs[-2:]
+        refs = refs[:-2]
+    else:
+        part, out = refs[:2]
+        refs = refs[2:]
+    if "cond" in axes:
+        landed, send, recv, mine, crossed, cross_send, cross_recv = refs
+    else:
+        landed, send, recv = refs
     count = lax.axis_size("slab")
-    head = cells[:width]
-    tail = cells[cells.shape[0] - width :]
-    return jnp.concatenate(
-        [
-            lax.ppermute(tail, "slab", [(i, (i + 1) % count) for i in range(count)]),
-            cells,
-            lax.ppermute(head, "slab", [((i + 1) % count, i) for i in range(count)]),
-        ],
-        axis=0,
-    )
+    me = lax.axis_index("slab")
+    conds = lax.axis_size("cond")
+    chunk = part.shape[0] // count
+    peer = [lax.rem(me + d, count) for d in range(count)]
+    rank = lax.axis_index("cond")
+
+    barrier = pltpu.get_barrier_semaphore()
+    for d in range(1, count):
+        pl.semaphore_signal(barrier, inc=1, device_id={"slab": peer[d]}, device_id_type=MESH)
+    waits = count - 1
+    if "cond" in axes:
+        for d in range(1, conds):
+            pl.semaphore_signal(
+                barrier, inc=1, device_id={"cond": lax.rem(rank + d, conds)}, device_id_type=MESH
+            )
+        waits += conds - 1
+    pl.semaphore_wait(barrier, waits)
+
+    def rows_of(owner):
+        return pl.ds(pl.multiple_of(owner * chunk, chunk), chunk)
+
+    first = [
+        pltpu.make_async_remote_copy(
+            src_ref=part.at[rows_of(peer[d])],
+            dst_ref=landed.at[d],
+            send_sem=send.at[0, d],
+            recv_sem=recv.at[0, d],
+            device_id={"slab": peer[d]},
+            device_id_type=MESH,
+        )
+        for d in range(1, count)
+    ]
+    for copy in first:
+        copy.start()
+    edges = []
+    if with_edges:
+        rows = diff.shape[0]
+        for number, (source, halo) in enumerate(((diff, diff_halo), (target, target_halo))):
+            for side, start, to in ((0, rows - HALO, 1), (1, 0, count - 1)):
+                at = 2 * number + side
+                edges.append(
+                    pltpu.make_async_remote_copy(
+                        src_ref=source.at[pl.ds(start, HALO)],
+                        dst_ref=halo.at[side],
+                        send_sem=edge_send.at[at],
+                        recv_sem=edge_recv.at[at],
+                        device_id={"slab": peer[to]},
+                        device_id_type=MESH,
+                    )
+                )
+        for copy in edges:
+            copy.start()
+    total = part[rows_of(me), :]
+    for d, copy in enumerate(first, 1):
+        copy.wait()
+        total = total + landed[d]
+    if "cond" in axes:
+        mine[...] = total
+        cross = [
+            pltpu.make_async_remote_copy(
+                src_ref=mine,
+                dst_ref=crossed.at[rank],
+                send_sem=cross_send.at[d],
+                recv_sem=cross_recv.at[d],
+                device_id={"cond": lax.rem(rank + d, conds)},
+                device_id_type=MESH,
+            )
+            for d in range(1, conds)
+        ]
+        for copy in cross:
+            copy.start()
+        crossed[rank] = total
+        for copy in cross:
+            copy.wait()
+        total = crossed[0]
+        for c in range(1, conds):
+            total = total + crossed[c]
+    out[rows_of(me), :] = total
+    second = [
+        pltpu.make_async_remote_copy(
+            src_ref=out.at[rows_of(me)],
+            dst_ref=out.at[rows_of(me)],
+            send_sem=send.at[1, d],
+            recv_sem=recv.at[1, d],
+            device_id={"slab": peer[d]},
+            device_id_type=MESH,
+        )
+        for d in range(1, count)
+    ]
+    for copy in second:
+        copy.start()
+    for copy in second + edges:
+        copy.wait()
+
+
+def summed(part, axes, edges=()):
+    count = lax.axis_size("slab")
+    conds = lax.axis_size("cond")
+    chunk = part.shape[0] // count
+    dma = pltpu.SemaphoreType.DMA
+    scratch = [pltpu.VMEM((count, chunk, part.shape[1]), f32), dma((2, count)), dma((2, count))]
+    if "cond" in axes:
+        scratch += [
+            pltpu.VMEM((chunk, part.shape[1]), f32),
+            pltpu.VMEM((conds, chunk, part.shape[1]), f32),
+            dma((conds,)),
+            dma((conds,)),
+        ]
+    if edges:
+        scratch += [dma((4,)), dma((4,))]
+    return pl.pallas_call(
+        functools.partial(sum_kernel, axes, bool(edges)),
+        out_shape=(shape(part.shape),)
+        + tuple(shape((2, HALO, e.shape[1]), e.dtype) for e in edges),
+        in_specs=[VMEM] + [ANY] * len(edges),
+        out_specs=(VMEM,) * (1 + len(edges)),
+        scratch_shapes=scratch,
+        compiler_params=pltpu.CompilerParams(
+            collective_id=len(axes), has_side_effects=True
+        ),
+        name="sum_" + "_".join(axes),
+    )(part, *edges)
 
 
 def shape(dims, kind=f32):
@@ -294,7 +456,6 @@
     small, large = angle_parts(length, band, 64)
     left = coarse_tables(band)
     lh, ll = split_np(left)
-    th, tl = split_np(np.ascontiguousarray(left.T))
     wh, wl = split_np(interpolation_table(length, band))
     trans, tab_h, tab_l, local = pl.pallas_call(
         project_kernel,
@@ -310,15 +471,11 @@
         compiler_params=params,
         name="project",
     )(mask_pixels, perturb, small, large)
-    mask_band = lax.psum(local, "slab")
-    levels = jnp.arange(dose_table.shape[0], dtype=jnp.int32)
-    dose = jnp.sum(dose_table * (levels == cond_ids[0]).astype(f32)).reshape(1, 1)
-    diff = with_halo(diffusivity, HALO)
-    target = with_halo(target_bits, HALO)
+    mask_band, diff_halo, target_halo = summed(local, ("slab",), (diffusivity, target_bits))
     part = pl.pallas_call(
         image_kernel,
         out_shape=shape((points, band)),
-        in_specs=[VMEM] * 2 + [SMEM] + [VMEM] * 8,
+        in_specs=[VMEM] * 2 + [SMEM] * 2 + [ANY] * 2 + [VMEM] * 6,
         out_specs=VMEM,
         scratch_shapes=[
             pltpu.VMEM((points, count * band), bf16),
@@ -326,6 +483,10 @@
             pltpu.VMEM((2 * points, count * band), f32),
             pltpu.VMEM((count, points, 2 * points), f32),
             pltpu.VMEM((points, points), f32),
+            pltpu.VMEM((total + 16, length), f32),
+            pltpu.VMEM((total + 16, length), f32),
+            pltpu.VMEM((total, length), f32),
+            pltpu.VMEM((total, length), f32),
             pltpu.VMEM((total, length), f32),
             pltpu.VMEM((total, length), f32),
             pltpu.VMEM((total, length), f32),
@@ -334,11 +495,19 @@
             pltpu.VMEM((rows, points), f32),
             pltpu.VMEM((2 * points, count * band), bf16),
             pltpu.VMEM((2 * points, count * band), bf16),
+            pltpu.VMEM((points, 2 * points), bf16),
+            pltpu.VMEM((points, 2 * points), bf16),
+            pltpu.VMEM((total + 16, length), f32),
+            pltpu.VMEM((total, length), jnp.int32),
+            pltpu.SemaphoreType.DMA((6,)),
         ],
         compiler_params=params,
         name="image",
-    )(mask_band, kernels[0], dose, diff, target, lh, ll, th, tl, wh, wl)
-    grad = lax.psum(part, ("cond", "slab"))
+    )(
+        mask_band, kernels[0], cond_ids, dose_table, diffusivity, target_bits,
+        diff_halo, target_halo, lh, ll, wh, wl,
+    )
+    (grad,) = summed(part, ("cond", "slab"))
     return pl.pallas_call(
         final_kernel,
         out_shape=shape((rows, length)),

time: 276 us -> 82.9 us (0.30)
  waiting for transfers between devices: 167 us -> 0 us
  between operations: 14.1 us -> 0.68 us
  starting transfers between devices: 8.27 us -> 0 us
  other arithmetic: 3.64 us -> 0 us
    psum x2 -> x0, waiting for transfers between devices: 167 us -> none  [the longest x1 124 us: shards(): grad = lax.psum(part, ('cond', 'slab'))]
    pallas_call x0 -> x2, Pallas kernels: none -> 33.9 us  [summed(): pl.pallas_call(functools.partial(sum_kernel, axes, bool(edges)), out_shap...]
    pallas_call x1, Pallas kernels: 67.3 us -> 34.9 us  [shards(): pl.pallas_call(image_kernel, out_shape=shape((points, band)), in_specs=[V...]
    ppermute x4 -> x0, starting transfers between devices: 8.23 us -> none  [the longest x2 7.62 us: with_halo(): lax.ppermute(head, 'slab', [((i + 1) % count, i) for i in range(count)])]
    concatenate x2 -> x0, other arithmetic: 3.01 us -> none  [with_halo(): jnp.concatenate([lax.ppermute(tail, 'slab', [(i, (i + 1) % count) for i i...]
  transfers between devices with their start and end apart: 6 -> 0, of which waited for: 2 -> 0; matrix products, arithmetic and copies ran while one was open for 2% -> 0% of each run, Pallas kernels for 0% -> 0%
where the time goes in v1:
time: 82.9 us; the launch traced here: 82.8 us
  Pallas kernels  82.1 us (99%)
    pallas_call x1, Pallas kernels, shards(): pl.pallas_call(image_kernel, out_shape=shape((points, band)), in_specs=[V...  34.9 us
    pallas_call x2, Pallas kernels, summed(): pl.pallas_call(functools.partial(sum_kernel, axes, bool(edges)), out_shap...  33.9 us
    pallas_call x1, Pallas kernels, shards(): pl.pallas_call(project_kernel, out_shape=(shape((rows, length)), shape((l...  7.04 us
    pallas_call x1, Pallas kernels, shards(): pl.pallas_call(final_kernel, out_shape=shape((rows, length)), in_specs=[V...  6.24 us

profile of v1, /device:TPU:0, one launch (start us, length us, event | category | flops | bytes accessed | tf_op | source)
XLA Modules:
  0.0 82.8 jit_solution(7558319882850268525)
XLA Ops:
  0.7 7.0 %project.1 = (f32[256,2048]{1,0:T(8,128)}, bf16[2048,256]{1,0:T(8,128)(2,1)}, bf16[2048,256]{1,0:T(8,128)(2,1)}, f32[256,128]{1,0:T(8,128)}) custom-call(s32[256,2048]{1,0:T(8,128)} %mask.1, f32[256,2048]{1,0:T(8,128)} %perturb.1, f32[2,64,128]{2,1,0:T(8,128)} %constant.12.clone.small, f32[2,32,128]{2,1,0:T(8,128)} %constant.13.clone.large), custom_call_target="tpu_custom_call" | custom-call | tf_op jit(solution)/shard_map/project/pallas_call | solution.py:460
  7.7 16.2 %sum_slab.1 = (f32[256,128]{1,0:T(8,128)}, f32[2,8,2048]{2,1,0:T(8,128)}, s32[2,8,2048]{2,1,0:T(8,128)}) custom-call(f32[256,128]{1,0:T(8,128)} %get-tuple-element.12.refs_0_, f32[256,2048]{1,0:T(8,128)} %diff.1, s32[256,2048]{1,0:T(8,128)} %target.1), custom_call_target="tpu_custom_call" | custom-call | tf_op jit(solution)/shard_map/sum_slab/pallas_call | solution.py:432
  23.9 34.9 %image.1.refs_0_ = f32[256,128]{1,0:T(8,128)} custom-call(f32[256,128]{1,0:T(8,128)} %get-tuple-element.13.band_in, f32[8,2,128,128]{3,2,1,0:T(8,128)} %bitcast.1, s32[1]{0:T(128)S(6)} %copy.14.ids, f32[16]{0:T(128)} %table.1, f32[256,2048]{1,0:T(8,128)} %diff.1, s32[256,2048]{1,0:T(8,128)} %target.1, f32[2,8,2048]{2,1,0:T(8,128)} %get-tuple-element.14.diff_halo, ...), custom_call_target="tpu_custom_call" | custom-call | tf_op jit(solution)/shard_map/image/pallas_call | solution.py:475
  58.8 17.7 %sum_cond_slab.1.grad = f32[256,128]{1,0:T(8,128)} custom-call(f32[256,128]{1,0:T(8,128)} %image.1.refs_0_), custom_call_target="tpu_custom_call" | custom-call | tf_op jit(solution)/shard_map/sum_cond_slab/pallas_call | solution.py:432
  76.5 6.2 %final.1 = f32[256,2048]{1,0:T(8,128)} custom-call(f32[256,128]{1,0:T(8,128)} %sum_cond_slab.1.grad, f32[256,2048]{1,0:T(8,128)} %get-tuple-element.16.trans, bf16[2048,256]{1,0:T(8,128)(2,1)} %get-tuple-element.17.tab_h, bf16[2048,256]{1,0:T(8,128)(2,1)} %get-tuple-element.18.tab_l), custom_call_target="tpu_custom_call" | custom-call | tf_op jit(solution)/shard_map/final/pallas_call | solution.py:511

commit v2 on v1

--- a/solution.py
+++ b/solution.py
@@ -437,7 +437,7 @@
         out_specs=(VMEM,) * (1 + len(edges)),
         scratch_shapes=scratch,
         compiler_params=pltpu.CompilerParams(
-            collective_id=len(axes), has_side_effects=True
+            collective_id=len(axes), has_side_effects=True, vmem_limit_bytes=4 * 1024 * 1024
         ),
         name="sum_" + "_".join(axes),
     )(part, *edges)
@@ -452,7 +452,8 @@
     count, band = kernels.shape[1], kernels.shape[-1]
     points = 2 * band
     total = rows + 2 * HALO
-    params = pltpu.CompilerParams(vmem_limit_bytes=60 * 1024 * 1024)
+    mib = 1024 * 1024
+    params = pltpu.CompilerParams(vmem_limit_bytes=12 * mib)
     small, large = angle_parts(length, band, 64)
     left = coarse_tables(band)
     lh, ll = split_np(left)
@@ -501,7 +502,7 @@
             pltpu.VMEM((total, length), jnp.int32),
             pltpu.SemaphoreType.DMA((6,)),
         ],
-        compiler_params=params,
+        compiler_params=pltpu.CompilerParams(vmem_limit_bytes=40 * mib),
         name="image",
     )(
         mask_band, kernels[0], cond_ids, dose_table, diffusivity, target_bits,

time: 82.9 us -> 77.2 us (0.931)
  Pallas kernels: 82.1 us -> 71.3 us
  local copies, waits for them, and re-layouts: 0 us -> 4.82 us
    unnamed x0 -> x24, local copies, waits for them, and re-layouts: none -> 4.82 us
    pallas_call x1, Pallas kernels: 7.04 us -> 3.39 us  [shards(): pl.pallas_call(project_kernel, out_shape=(shape((rows, length)), shape((l...]
    pallas_call x2, Pallas kernels: 33.9 us -> 30.8 us  [summed(): pl.pallas_call(functools.partial(sum_kernel, axes, bool(edges)), out_shap...]
    pallas_call x1, Pallas kernels: 6.24 us -> 4.03 us  [shards(): pl.pallas_call(final_kernel, out_shape=shape((rows, length)), in_specs=[V...]
    pallas_call x1, Pallas kernels: 34.9 us -> 33 us  [shards(): pl.pallas_call(image_kernel, out_shape=shape((points, band)), in_specs=[V...]
where the time goes in v2:
time: 77.2 us; the launch traced here: 76.9 us
  Pallas kernels  71.3 us (92%)
  local copies, waits for them, and re-layouts  4.82 us (6%)
  between operations  0.81 us (1%)
    pallas_call x1, Pallas kernels, shards(): pl.pallas_call(image_kernel, out_shape=shape((points, band)), in_specs=[V...  33 us
    pallas_call x2, Pallas kernels, summed(): pl.pallas_call(functools.partial(sum_kernel, axes, bool(edges)), out_shap...  30.8 us
    unnamed x24, local copies, waits for them, and re-layouts  4.82 us
    pallas_call x1, Pallas kernels, shards(): pl.pallas_call(final_kernel, out_shape=shape((rows, length)), in_specs=[V...  4.03 us
    pallas_call x1, Pallas kernels, shards(): pl.pallas_call(project_kernel, out_shape=(shape((rows, length)), shape((l...  3.39 us

profile of v2, /device:TPU:0, one launch (start us, length us, event | category | flops | bytes accessed | tf_op | source)
XLA Modules:
  0.0 76.9 jit_solution(13131872134358435454)
XLA Ops:
  0.7 0.0 copy-start.2
  0.7 1.6 %copy-done.2 = s32[256,2048]{1,0:T(8,128)S(1)} copy-done((s32[256,2048]{1,0:T(8,128)S(1)}, s32[256,2048]{1,0:T(8,128)}, u32[]{:S(2)}) %copy-start.2) | copy-done | bytes 2097176
  2.2 0.0 copy-start.3
  2.2 1.6 %copy-done.3 = f32[256,2048]{1,0:T(8,128)S(1)} copy-done((f32[256,2048]{1,0:T(8,128)S(1)}, f32[256,2048]{1,0:T(8,128)}, u32[]{:S(2)}) %copy-start.3) | copy-done | bytes 2097176
  3.8 0.0 copy-start.9
  3.8 0.8 %copy-done.9 = f32[2,64,128]{2,1,0:T(8,128)S(1)} copy-done((f32[2,64,128]{2,1,0:T(8,128)S(1)}, f32[2,64,128]{2,1,0:T(8,128)}, u32[]{:S(2)}) %copy-start.9) | copy-done | bytes 65560
  4.7 0.0 copy-start.10
  4.7 0.8 copy-done.10
  5.4 0.0 copy-start
  5.4 0.0 copy-start.1
  5.4 3.4 %project.1 = (f32[256,2048]{1,0:T(8,128)S(1)}, bf16[2048,256]{1,0:T(8,128)(2,1)S(1)}, bf16[2048,256]{1,0:T(8,128)(2,1)S(1)}, f32[256,128]{1,0:T(8,128)S(1)}) custom-call(s32[256,2048]{1,0:T(8,128)S(1)} %copy-done.2, f32[256,2048]{1,0:T(8,128)S(1)} %copy-done.3, f32[2,64,128]{2,1,0:T(8,128)S(1)} %copy-done.9, f32[2,32,128]{2,1,0:T(8,128)S(1)} %copy-done.10), custom_call_target="tpu_custom_call" | custom-call | tf_op jit(solution)/shard_map/project/pallas_call | solution.py:461
  8.8 0.0 copy-done
  8.8 0.0 copy-done.1
  8.9 0.0 copy-start.4
  8.9 0.0 copy-start.5
  8.9 0.0 copy-start.6
  8.9 0.0 copy-start.7
  8.9 0.0 copy-start.8
  8.9 0.0 copy-start.11
  8.9 14.6 %sum_slab.1 = (f32[256,128]{1,0:T(8,128)S(1)}, f32[2,8,2048]{2,1,0:T(8,128)S(1)}, s32[2,8,2048]{2,1,0:T(8,128)S(1)}) custom-call(f32[256,128]{1,0:T(8,128)S(1)} %get-tuple-element.12.refs_0_, f32[256,2048]{1,0:T(8,128)S(1)} %copy-done, s32[256,2048]{1,0:T(8,128)S(1)} %copy-done.1), custom_call_target="tpu_custom_call" | custom-call | tf_op jit(solution)/shard_map/sum_slab/pallas_call | solution.py:432
  23.6 0.0 copy-done.4
  23.6 0.0 copy-done.5
  23.6 0.0 copy-done.6
  23.6 0.0 copy-done.7
  23.6 0.0 copy-done.8
  23.6 0.0 copy-done.11
  23.6 33.0 %image.1.refs_0_ = f32[256,128]{1,0:T(8,128)S(1)} custom-call(f32[256,128]{1,0:T(8,128)S(1)} %get-tuple-element.13.band_in, f32[8,2,128,128]{3,2,1,0:T(8,128)S(1)} %bitcast.1, s32[1]{0:T(128)S(6)} %copy.14.ids, f32[16]{0:T(128)S(1)} %copy-done.11, f32[256,2048]{1,0:T(8,128)S(1)} %copy-done, s32[256,2048]{1,0:T(8,128)S(1)} %copy-done.1, ...), custom_call_target="tpu_custom_call" | custom-call | tf_op jit(solution)/shard_map/image/pallas_call | solution.py:476
  56.7 16.2 %sum_cond_slab.1.grad = f32[256,128]{1,0:T(8,128)S(1)} custom-call(f32[256,128]{1,0:T(8,128)S(1)} %image.1.refs_0_), custom_call_target="tpu_custom_call" | custom-call | tf_op jit(solution)/shard_map/sum_cond_slab/pallas_call | solution.py:432
  72.9 4.0 %final.1 = f32[256,2048]{1,0:T(8,128)} custom-call(f32[256,128]{1,0:T(8,128)S(1)} %sum_cond_slab.1.grad, f32[256,2048]{1,0:T(8,128)S(1)} %get-tuple-element.16.trans, bf16[2048,256]{1,0:T(8,128)(2,1)S(1)} %get-tuple-element.17.tab_h, bf16[2048,256]{1,0:T(8,128)(2,1)S(1)} %get-tuple-element.18.tab_l), custom_call_target="tpu_custom_call" | custom-call | tf_op jit(solution)/shard_map/final/pallas_call | solution.py:512
Async XLA Ops:
  0.7 1.6 %copy-start.2 = (s32[256,2048]{1,0:T(8,128)S(1)}, s32[256,2048]{1,0:T(8,128)}, u32[]{:S(2)}) copy-start(s32[256,2048]{1,0:T(8,128)} %mask.1) | copy-start | bytes 6291460
  2.2 1.6 %copy-start.3 = (f32[256,2048]{1,0:T(8,128)S(1)}, f32[256,2048]{1,0:T(8,128)}, u32[]{:S(2)}) copy-start(f32[256,2048]{1,0:T(8,128)} %perturb.1) | copy-start | bytes 6291460
  3.8 0.8 %copy-start.9 = (f32[2,64,128]{2,1,0:T(8,128)S(1)}, f32[2,64,128]{2,1,0:T(8,128)}, u32[]{:S(2)}) copy-start(f32[2,64,128]{2,1,0:T(8,128)} %constant.12.clone.small) | copy-start | bytes 196612
  4.7 0.8 copy-start.10
  5.4 3.4 %copy-start = (f32[256,2048]{1,0:T(8,128)S(1)}, f32[256,2048]{1,0:T(8,128)}, u32[]{:S(2)}) copy-start(f32[256,2048]{1,0:T(8,128)} %diff.1) | copy-start | bytes 6291460
  5.4 3.4 %copy-start.1 = (s32[256,2048]{1,0:T(8,128)S(1)}, s32[256,2048]{1,0:T(8,128)}, u32[]{:S(2)}) copy-start(s32[256,2048]{1,0:T(8,128)} %target.1) | copy-start | bytes 6291460
  8.9 14.7 %copy-start.4 = (bf16[2064,256]{1,0:T(8,128)(2,1)S(1)}, bf16[2064,256]{1,0:T(8,128)(2,1)}, u32[]{:S(2)}) copy-start(bf16[2064,256]{1,0:T(8,128)(2,1)} %constant.17.clone.wl) | copy-start | bytes 3170308
  8.9 14.7 %copy-start.5 = (bf16[2064,256]{1,0:T(8,128)(2,1)S(1)}, bf16[2064,256]{1,0:T(8,128)(2,1)}, u32[]{:S(2)}) copy-start(bf16[2064,256]{1,0:T(8,128)(2,1)} %constant.16.clone.wh) | copy-start | bytes 3170308
  8.9 14.7 %copy-start.6 = (f32[1,8,2,128,128]{4,3,2,1,0:T(8,128)S(1)}, f32[1,8,2,128,128]{4,3,2,1,0:T(8,128)}, u32[]{:S(2)}) copy-start(f32[1,8,2,128,128]{4,3,2,1,0:T(8,128)} %param.17) | copy-start | bytes 3145732
  8.9 14.7 %copy-start.7 = (bf16[512,256]{1,0:T(8,128)(2,1)S(1)}, bf16[512,256]{1,0:T(8,128)(2,1)}, u32[]{:S(2)}) copy-start(bf16[512,256]{1,0:T(8,128)(2,1)} %constant.15.clone.ll) | copy-start | bytes 786436
  8.9 14.7 %copy-start.8 = (bf16[512,256]{1,0:T(8,128)(2,1)S(1)}, bf16[512,256]{1,0:T(8,128)(2,1)}, u32[]{:S(2)}) copy-start(bf16[512,256]{1,0:T(8,128)(2,1)} %constant.14.clone.lh) | copy-start | bytes 786436
  8.9 14.7 %copy-start.11 = (f32[16]{0:T(128)S(1)}, f32[16]{0:T(128)}, u32[]{:S(2)}) copy-start(f32[16]{0:T(128)} %table.1) | copy-start | bytes 196

commit v3 on v2

--- a/solution.py
+++ b/solution.py
@@ -414,13 +414,102 @@
         copy.wait()
 
 
+def flat_kernel(axes, with_edges, *refs):
+    if with_edges:
+        part, diff, target, out, diff_halo, target_halo, landed, send, recv, edge_send, edge_recv = refs
+    else:
+        part, out, landed, send, recv = refs
+    count = lax.axis_size("slab")
+    conds = lax.axis_size("cond")
+    me = lax.axis_index("slab")
+    rank = lax.axis_index("cond")
+    chunk = part.shape[0] // (count * conds)
+    peer = [lax.rem(me + d, count) for d in range(count)]
+    others = [(c, d) for c in range(conds) for d in range(count) if c or d]
+
+    def place(c, d):
+        return {"cond": lax.rem(rank + c, conds), "slab": lax.rem(me + d, count)}
+
+    def rows_of(where):
+        owner = where["slab"] * conds + where["cond"]
+        return pl.ds(pl.multiple_of(owner * chunk, chunk), chunk)
+
+    barrier = pltpu.get_barrier_semaphore()
+    for c, d in others:
+        pl.semaphore_signal(barrier, inc=1, device_id=place(c, d), device_id_type=MESH)
+    pl.semaphore_wait(barrier, len(others))
+
+    adders = others if "cond" in axes else [(c, d) for c, d in others if c == 0]
+    first = []
+    for c, d in adders:
+        first.append(
+            pltpu.make_async_remote_copy(
+                src_ref=part.at[rows_of(place(c, d))],
+                dst_ref=landed.at[c * count + d],
+                send_sem=send.at[0, c * count + d],
+                recv_sem=recv.at[0, c * count + d],
+                device_id=place(c, d),
+                device_id_type=MESH,
+            )
+        )
+    for copy in first:
+        copy.start()
+    edges = []
+    if with_edges:
+        rows = diff.shape[0]
+        for number, (source, halo) in enumerate(((diff, diff_halo), (target, target_halo))):
+            for side, start, to in ((0, rows - HALO, 1), (1, 0, count - 1)):
+                at = 2 * number + side
+                edges.append(
+                    pltpu.make_async_remote_copy(
+                        src_ref=source.at[pl.ds(start, HALO)],
+                        dst_ref=halo.at[side],
+                        send_sem=edge_send.at[at],
+                        recv_sem=edge_recv.at[at],
+                        device_id={"slab": peer[to]},
+                        device_id_type=MESH,
+                    )
+                )
+        for copy in edges:
+            copy.start()
+    mine = rows_of(place(0, 0))
+    total = part[mine, :]
+    for (c, d), copy in zip(adders, first):
+        copy.wait()
+        total = total + landed[c * count + d]
+    out[mine, :] = total
+    second = [
+        pltpu.make_async_remote_copy(
+            src_ref=out.at[mine],
+            dst_ref=out.at[mine],
+            send_sem=send.at[1, c * count + d],
+            recv_sem=recv.at[1, c * count + d],
+            device_id=place(c, d),
+            device_id_type=MESH,
+        )
+        for c, d in others
+    ]
+    for copy in second:
+        copy.start()
+    for copy in second + edges:
+        copy.wait()
+
+
 def summed(part, axes, edges=()):
     count = lax.axis_size("slab")
     conds = lax.axis_size("cond")
     chunk = part.shape[0] // count
     dma = pltpu.SemaphoreType.DMA
     scratch = [pltpu.VMEM((count, chunk, part.shape[1]), f32), dma((2, count)), dma((2, count))]
-    if "cond" in axes:
+    flat = part.shape[0] % (8 * count * conds) == 0
+    if flat:
+        owners = count * conds
+        scratch = [
+            pltpu.VMEM((owners, part.shape[0] // owners, part.shape[1]), f32),
+            dma((2, owners)),
+            dma((2, owners)),
+        ]
+    elif "cond" in axes:
         scratch += [
             pltpu.VMEM((chunk, part.shape[1]), f32),
             pltpu.VMEM((conds, chunk, part.shape[1]), f32),
@@ -430,7 +519,7 @@
     if edges:
         scratch += [dma((4,)), dma((4,))]
     return pl.pallas_call(
-        functools.partial(sum_kernel, axes, bool(edges)),
+        functools.partial(flat_kernel if flat else sum_kernel, axes, bool(edges)),
         out_shape=(shape(part.shape),)
         + tuple(shape((2, HALO, e.shape[1]), e.dtype) for e in edges),
         in_specs=[VMEM] + [ANY] * len(edges),

time: 77.2 us -> 79.3 us (1.027)
  Pallas kernels: 71.3 us -> 73.4 us
    pallas_call x2, Pallas kernels: 30.8 us -> 32.9 us  [summed(): pl.pallas_call(functools.partial(flat_kernel if flat else sum_kernel, axe...]
where the time goes in v3:
time: 79.3 us; the launch traced here: 79 us
  Pallas kernels  73.4 us (93%)
  local copies, waits for them, and re-layouts  4.82 us (6%)
  between operations  0.81 us (1%)
    pallas_call x1, Pallas kernels, shards(): pl.pallas_call(image_kernel, out_shape=shape((points, band)), in_specs=[V...  33 us
    pallas_call x2, Pallas kernels, summed(): pl.pallas_call(functools.partial(flat_kernel if flat else sum_kernel, axe...  32.9 us
    unnamed x24, local copies, waits for them, and re-layouts  4.82 us
    pallas_call x1, Pallas kernels, shards(): pl.pallas_call(final_kernel, out_shape=shape((rows, length)), in_specs=[V...  4.03 us
    pallas_call x1, Pallas kernels, shards(): pl.pallas_call(project_kernel, out_shape=(shape((rows, length)), shape((l...  3.39 us

profile of v3, /device:TPU:0, one launch (start us, length us, event | category | flops | bytes accessed | tf_op | source)
XLA Modules:
  0.0 79.0 jit_solution(3130375337685922490)
XLA Ops:
  0.7 0.0 copy-start.2
  0.7 1.6 %copy-done.2 = s32[256,2048]{1,0:T(8,128)S(1)} copy-done((s32[256,2048]{1,0:T(8,128)S(1)}, s32[256,2048]{1,0:T(8,128)}, u32[]{:S(2)}) %copy-start.2) | copy-done | bytes 2097176
  2.2 0.0 copy-start.3
  2.2 1.6 %copy-done.3 = f32[256,2048]{1,0:T(8,128)S(1)} copy-done((f32[256,2048]{1,0:T(8,128)S(1)}, f32[256,2048]{1,0:T(8,128)}, u32[]{:S(2)}) %copy-start.3) | copy-done | bytes 2097176
  3.8 0.0 copy-start.9
  3.8 0.8 %copy-done.9 = f32[2,64,128]{2,1,0:T(8,128)S(1)} copy-done((f32[2,64,128]{2,1,0:T(8,128)S(1)}, f32[2,64,128]{2,1,0:T(8,128)}, u32[]{:S(2)}) %copy-start.9) | copy-done | bytes 65560
  4.7 0.0 copy-start.10
  4.7 0.8 copy-done.10
  5.4 0.0 copy-start
  5.4 0.0 copy-start.1
  5.4 3.4 %project.1 = (f32[256,2048]{1,0:T(8,128)S(1)}, bf16[2048,256]{1,0:T(8,128)(2,1)S(1)}, bf16[2048,256]{1,0:T(8,128)(2,1)S(1)}, f32[256,128]{1,0:T(8,128)S(1)}) custom-call(s32[256,2048]{1,0:T(8,128)S(1)} %copy-done.2, f32[256,2048]{1,0:T(8,128)S(1)} %copy-done.3, f32[2,64,128]{2,1,0:T(8,128)S(1)} %copy-done.9, f32[2,32,128]{2,1,0:T(8,128)S(1)} %copy-done.10), custom_call_target="tpu_custom_call" | custom-call | tf_op jit(solution)/shard_map/project/pallas_call | solution.py:550
  8.8 0.0 copy-done
  8.8 0.0 copy-done.1
  8.9 0.0 copy-start.4
  8.9 0.0 copy-start.5
  8.9 0.0 copy-start.6
  8.9 0.0 copy-start.7
  8.9 0.0 copy-start.8
  8.9 0.0 copy-start.11
  8.9 17.1 %sum_slab.1 = (f32[256,128]{1,0:T(8,128)S(1)}, f32[2,8,2048]{2,1,0:T(8,128)S(1)}, s32[2,8,2048]{2,1,0:T(8,128)S(1)}) custom-call(f32[256,128]{1,0:T(8,128)S(1)} %get-tuple-element.12.refs_0_, f32[256,2048]{1,0:T(8,128)S(1)} %copy-done, s32[256,2048]{1,0:T(8,128)S(1)} %copy-done.1), custom_call_target="tpu_custom_call" | custom-call | tf_op jit(solution)/shard_map/sum_slab/pallas_call | solution.py:521
  26.0 0.0 copy-done.4
  26.0 0.0 copy-done.5
  26.0 0.0 copy-done.6
  26.0 0.0 copy-done.7
  26.1 0.0 copy-done.8
  26.1 0.0 copy-done.11
  26.1 33.0 %image.1.refs_0_ = f32[256,128]{1,0:T(8,128)S(1)} custom-call(f32[256,128]{1,0:T(8,128)S(1)} %get-tuple-element.13.band_in, f32[8,2,128,128]{3,2,1,0:T(8,128)S(1)} %bitcast.1, s32[1]{0:T(128)S(6)} %copy.14.ids, f32[16]{0:T(128)S(1)} %copy-done.11, f32[256,2048]{1,0:T(8,128)S(1)} %copy-done, s32[256,2048]{1,0:T(8,128)S(1)} %copy-done.1, ...), custom_call_target="tpu_custom_call" | custom-call | tf_op jit(solution)/shard_map/image/pallas_call | solution.py:565
  59.1 15.8 %sum_cond_slab.1.grad = f32[256,128]{1,0:T(8,128)S(1)} custom-call(f32[256,128]{1,0:T(8,128)S(1)} %image.1.refs_0_), custom_call_target="tpu_custom_call" | custom-call | tf_op jit(solution)/shard_map/sum_cond_slab/pallas_call | solution.py:521
  75.0 4.0 %final.1 = f32[256,2048]{1,0:T(8,128)} custom-call(f32[256,128]{1,0:T(8,128)S(1)} %sum_cond_slab.1.grad, f32[256,2048]{1,0:T(8,128)S(1)} %get-tuple-element.16.trans, bf16[2048,256]{1,0:T(8,128)(2,1)S(1)} %get-tuple-element.17.tab_h, bf16[2048,256]{1,0:T(8,128)(2,1)S(1)} %get-tuple-element.18.tab_l), custom_call_target="tpu_custom_call" | custom-call | tf_op jit(solution)/shard_map/final/pallas_call | solution.py:601
Async XLA Ops:
  0.7 1.6 %copy-start.2 = (s32[256,2048]{1,0:T(8,128)S(1)}, s32[256,2048]{1,0:T(8,128)}, u32[]{:S(2)}) copy-start(s32[256,2048]{1,0:T(8,128)} %mask.1) | copy-start | bytes 6291460
  2.2 1.6 %copy-start.3 = (f32[256,2048]{1,0:T(8,128)S(1)}, f32[256,2048]{1,0:T(8,128)}, u32[]{:S(2)}) copy-start(f32[256,2048]{1,0:T(8,128)} %perturb.1) | copy-start | bytes 6291460
  3.8 0.8 %copy-start.9 = (f32[2,64,128]{2,1,0:T(8,128)S(1)}, f32[2,64,128]{2,1,0:T(8,128)}, u32[]{:S(2)}) copy-start(f32[2,64,128]{2,1,0:T(8,128)} %constant.12.clone.small) | copy-start | bytes 196612
  4.7 0.8 copy-start.10
  5.4 3.4 %copy-start = (f32[256,2048]{1,0:T(8,128)S(1)}, f32[256,2048]{1,0:T(8,128)}, u32[]{:S(2)}) copy-start(f32[256,2048]{1,0:T(8,128)} %diff.1) | copy-start | bytes 6291460
  5.4 3.4 %copy-start.1 = (s32[256,2048]{1,0:T(8,128)S(1)}, s32[256,2048]{1,0:T(8,128)}, u32[]{:S(2)}) copy-start(s32[256,2048]{1,0:T(8,128)} %target.1) | copy-start | bytes 6291460
  8.9 17.2 %copy-start.4 = (bf16[2064,256]{1,0:T(8,128)(2,1)S(1)}, bf16[2064,256]{1,0:T(8,128)(2,1)}, u32[]{:S(2)}) copy-start(bf16[2064,256]{1,0:T(8,128)(2,1)} %constant.17.clone.wl) | copy-start | bytes 3170308
  8.9 17.2 %copy-start.5 = (bf16[2064,256]{1,0:T(8,128)(2,1)S(1)}, bf16[2064,256]{1,0:T(8,128)(2,1)}, u32[]{:S(2)}) copy-start(bf16[2064,256]{1,0:T(8,128)(2,1)} %constant.16.clone.wh) | copy-start | bytes 3170308
  8.9 17.2 %copy-start.6 = (f32[1,8,2,128,128]{4,3,2,1,0:T(8,128)S(1)}, f32[1,8,2,128,128]{4,3,2,1,0:T(8,128)}, u32[]{:S(2)}) copy-start(f32[1,8,2,128,128]{4,3,2,1,0:T(8,128)} %param.17) | copy-start | bytes 3145732
  8.9 17.2 %copy-start.7 = (bf16[512,256]{1,0:T(8,128)(2,1)S(1)}, bf16[512,256]{1,0:T(8,128)(2,1)}, u32[]{:S(2)}) copy-start(bf16[512,256]{1,0:T(8,128)(2,1)} %constant.15.clone.ll) | copy-start | bytes 786436
  8.9 17.1 %copy-start.8 = (bf16[512,256]{1,0:T(8,128)(2,1)S(1)}, bf16[512,256]{1,0:T(8,128)(2,1)}, u32[]{:S(2)}) copy-start(bf16[512,256]{1,0:T(8,128)(2,1)} %constant.14.clone.lh) | copy-start | bytes 786436
  8.9 17.1 %copy-start.11 = (f32[16]{0:T(128)S(1)}, f32[16]{0:T(128)}, u32[]{:S(2)}) copy-start(f32[16]{0:T(128)} %table.1) | copy-start | bytes 196

commit v4 on v3

--- a/solution.py
+++ b/solution.py
@@ -501,7 +501,7 @@
     chunk = part.shape[0] // count
     dma = pltpu.SemaphoreType.DMA
     scratch = [pltpu.VMEM((count, chunk, part.shape[1]), f32), dma((2, count)), dma((2, count))]
-    flat = part.shape[0] % (8 * count * conds) == 0
+    flat = "cond" in axes and part.shape[0] % (8 * count * conds) == 0
     if flat:
         owners = count * conds
         scratch = [

time: 79.3 us -> 78.2 us (0.986)
  Pallas kernels: 73.4 us -> 72.3 us
    pallas_call x2, Pallas kernels: 32.9 us -> 31.8 us  [summed(): pl.pallas_call(functools.partial(flat_kernel if flat else sum_kernel, axe...]
where the time goes in v4:
time: 78.2 us; the launch traced here: 77.9 us
  Pallas kernels  72.3 us (92%)
  local copies, waits for them, and re-layouts  4.82 us (6%)
  between operations  0.81 us (1%)
    pallas_call x1, Pallas kernels, shards(): pl.pallas_call(image_kernel, out_shape=shape((points, band)), in_specs=[V...  33 us
    pallas_call x2, Pallas kernels, summed(): pl.pallas_call(functools.partial(flat_kernel if flat else sum_kernel, axe...  31.8 us
    unnamed x24, local copies, waits for them, and re-layouts  4.82 us
    pallas_call x1, Pallas kernels, shards(): pl.pallas_call(final_kernel, out_shape=shape((rows, length)), in_specs=[V...  4.03 us
    pallas_call x1, Pallas kernels, shards(): pl.pallas_call(project_kernel, out_shape=(shape((rows, length)), shape((l...  3.39 us

profile of v4, /device:TPU:0, one launch (start us, length us, event | category | flops | bytes accessed | tf_op | source)
XLA Modules:
  0.0 77.9 jit_solution(16745304768561008542)
XLA Ops:
  0.7 0.0 copy-start.2
  0.7 1.6 %copy-done.2 = s32[256,2048]{1,0:T(8,128)S(1)} copy-done((s32[256,2048]{1,0:T(8,128)S(1)}, s32[256,2048]{1,0:T(8,128)}, u32[]{:S(2)}) %copy-start.2) | copy-done | bytes 2097176
  2.2 0.0 copy-start.3
  2.2 1.6 %copy-done.3 = f32[256,2048]{1,0:T(8,128)S(1)} copy-done((f32[256,2048]{1,0:T(8,128)S(1)}, f32[256,2048]{1,0:T(8,128)}, u32[]{:S(2)}) %copy-start.3) | copy-done | bytes 2097176
  3.8 0.0 copy-start.9
  3.8 0.8 %copy-done.9 = f32[2,64,128]{2,1,0:T(8,128)S(1)} copy-done((f32[2,64,128]{2,1,0:T(8,128)S(1)}, f32[2,64,128]{2,1,0:T(8,128)}, u32[]{:S(2)}) %copy-start.9) | copy-done | bytes 65560
  4.7 0.0 copy-start.10
  4.7 0.8 copy-done.10
  5.4 0.0 copy-start
  5.4 0.0 copy-start.1
  5.4 3.4 %project.1 = (f32[256,2048]{1,0:T(8,128)S(1)}, bf16[2048,256]{1,0:T(8,128)(2,1)S(1)}, bf16[2048,256]{1,0:T(8,128)(2,1)S(1)}, f32[256,128]{1,0:T(8,128)S(1)}) custom-call(s32[256,2048]{1,0:T(8,128)S(1)} %copy-done.2, f32[256,2048]{1,0:T(8,128)S(1)} %copy-done.3, f32[2,64,128]{2,1,0:T(8,128)S(1)} %copy-done.9, f32[2,32,128]{2,1,0:T(8,128)S(1)} %copy-done.10), custom_call_target="tpu_custom_call" | custom-call | tf_op jit(solution)/shard_map/project/pallas_call | solution.py:550
  8.8 0.0 copy-done
  8.8 0.0 copy-done.1
  8.9 0.0 copy-start.4
  8.9 0.0 copy-start.5
  8.9 0.0 copy-start.6
  8.9 0.0 copy-start.7
  8.9 0.0 copy-start.8
  8.9 0.0 copy-start.11
  8.9 14.6 %sum_slab.1 = (f32[256,128]{1,0:T(8,128)S(1)}, f32[2,8,2048]{2,1,0:T(8,128)S(1)}, s32[2,8,2048]{2,1,0:T(8,128)S(1)}) custom-call(f32[256,128]{1,0:T(8,128)S(1)} %get-tuple-element.12.refs_0_, f32[256,2048]{1,0:T(8,128)S(1)} %copy-done, s32[256,2048]{1,0:T(8,128)S(1)} %copy-done.1), custom_call_target="tpu_custom_call" | custom-call | tf_op jit(solution)/shard_map/sum_slab/pallas_call | solution.py:521
  23.6 0.0 copy-done.4
  23.6 0.0 copy-done.5
  23.6 0.0 copy-done.6
  23.6 0.0 copy-done.7
  23.6 0.0 copy-done.8
  23.6 0.0 copy-done.11
  23.6 33.0 %image.1.refs_0_ = f32[256,128]{1,0:T(8,128)S(1)} custom-call(f32[256,128]{1,0:T(8,128)S(1)} %get-tuple-element.13.band_in, f32[8,2,128,128]{3,2,1,0:T(8,128)S(1)} %bitcast.1, s32[1]{0:T(128)S(6)} %copy.14.ids, f32[16]{0:T(128)S(1)} %copy-done.11, f32[256,2048]{1,0:T(8,128)S(1)} %copy-done, s32[256,2048]{1,0:T(8,128)S(1)} %copy-done.1, ...), custom_call_target="tpu_custom_call" | custom-call | tf_op jit(solution)/shard_map/image/pallas_call | solution.py:565
  56.7 17.2 %sum_cond_slab.1.grad = f32[256,128]{1,0:T(8,128)S(1)} custom-call(f32[256,128]{1,0:T(8,128)S(1)} %image.1.refs_0_), custom_call_target="tpu_custom_call" | custom-call | tf_op jit(solution)/shard_map/sum_cond_slab/pallas_call | solution.py:521
  73.9 4.0 %final.1 = f32[256,2048]{1,0:T(8,128)} custom-call(f32[256,128]{1,0:T(8,128)S(1)} %sum_cond_slab.1.grad, f32[256,2048]{1,0:T(8,128)S(1)} %get-tuple-element.16.trans, bf16[2048,256]{1,0:T(8,128)(2,1)S(1)} %get-tuple-element.17.tab_h, bf16[2048,256]{1,0:T(8,128)(2,1)S(1)} %get-tuple-element.18.tab_l), custom_call_target="tpu_custom_call" | custom-call | tf_op jit(solution)/shard_map/final/pallas_call | solution.py:601
Async XLA Ops:
  0.7 1.6 %copy-start.2 = (s32[256,2048]{1,0:T(8,128)S(1)}, s32[256,2048]{1,0:T(8,128)}, u32[]{:S(2)}) copy-start(s32[256,2048]{1,0:T(8,128)} %mask.1) | copy-start | bytes 6291460
  2.2 1.6 %copy-start.3 = (f32[256,2048]{1,0:T(8,128)S(1)}, f32[256,2048]{1,0:T(8,128)}, u32[]{:S(2)}) copy-start(f32[256,2048]{1,0:T(8,128)} %perturb.1) | copy-start | bytes 6291460
  3.8 0.8 %copy-start.9 = (f32[2,64,128]{2,1,0:T(8,128)S(1)}, f32[2,64,128]{2,1,0:T(8,128)}, u32[]{:S(2)}) copy-start(f32[2,64,128]{2,1,0:T(8,128)} %constant.12.clone.small) | copy-start | bytes 196612
  4.7 0.8 copy-start.10
  5.4 3.4 %copy-start = (f32[256,2048]{1,0:T(8,128)S(1)}, f32[256,2048]{1,0:T(8,128)}, u32[]{:S(2)}) copy-start(f32[256,2048]{1,0:T(8,128)} %diff.1) | copy-start | bytes 6291460
  5.4 3.4 %copy-start.1 = (s32[256,2048]{1,0:T(8,128)S(1)}, s32[256,2048]{1,0:T(8,128)}, u32[]{:S(2)}) copy-start(s32[256,2048]{1,0:T(8,128)} %target.1) | copy-start | bytes 6291460
  8.9 14.7 %copy-start.4 = (bf16[2064,256]{1,0:T(8,128)(2,1)S(1)}, bf16[2064,256]{1,0:T(8,128)(2,1)}, u32[]{:S(2)}) copy-start(bf16[2064,256]{1,0:T(8,128)(2,1)} %constant.17.clone.wl) | copy-start | bytes 3170308
  8.9 14.7 %copy-start.5 = (bf16[2064,256]{1,0:T(8,128)(2,1)S(1)}, bf16[2064,256]{1,0:T(8,128)(2,1)}, u32[]{:S(2)}) copy-start(bf16[2064,256]{1,0:T(8,128)(2,1)} %constant.16.clone.wh) | copy-start | bytes 3170308
  8.9 14.7 %copy-start.6 = (f32[1,8,2,128,128]{4,3,2,1,0:T(8,128)S(1)}, f32[1,8,2,128,128]{4,3,2,1,0:T(8,128)}, u32[]{:S(2)}) copy-start(f32[1,8,2,128,128]{4,3,2,1,0:T(8,128)} %param.17) | copy-start | bytes 3145732
  8.9 14.7 %copy-start.7 = (bf16[512,256]{1,0:T(8,128)(2,1)S(1)}, bf16[512,256]{1,0:T(8,128)(2,1)}, u32[]{:S(2)}) copy-start(bf16[512,256]{1,0:T(8,128)(2,1)} %constant.15.clone.ll) | copy-start | bytes 786436
  8.9 14.7 %copy-start.8 = (bf16[512,256]{1,0:T(8,128)(2,1)S(1)}, bf16[512,256]{1,0:T(8,128)(2,1)}, u32[]{:S(2)}) copy-start(bf16[512,256]{1,0:T(8,128)(2,1)} %constant.14.clone.lh) | copy-start | bytes 786436
  8.9 14.7 %copy-start.11 = (f32[16]{0:T(128)S(1)}, f32[16]{0:T(128)}, u32[]{:S(2)}) copy-start(f32[16]{0:T(128)} %table.1) | copy-start | bytes 196
